TPU v7x, 256 devices: a whole 4x4x8 slice. The times are simulated.
256 devices in a mesh: req: 32 (over z, x), tp: 8 (over y, core).
Axes of the slice: x: 4, y: 4, z: 8, core: 2. Of those that a mesh axis runs over, the one named last changes fastest.
Arguments:
- hidden_in: bfloat16 [192, 64, 3072], P('req', None, 'tp'), may hold values from -3 to 3
- request_order: int32 [192], replicated, may hold values from 0 to 191, as said below
- norm_gain: bfloat16 [3072], replicated, may hold values from 0.099609375 to 1.8984375
- w_query: bfloat16 [3072, 3072], P(None, 'tp'), may hold values from -0.109375 to 0.109375
- key_weight: bfloat16 [3072, 1024], P(None, 'tp'), may hold values from -0.4375 to 0.4375
- value_weight: bfloat16 [3072, 1024], P(None, 'tp'), may hold values from -0.109375 to 0.109375
- w_out: bfloat16 [3072, 3072], P('tp'), may hold values from -0.109375 to 0.109375
- key_cache: bfloat16 [192, 8, 3456, 128], P('req', 'tp'), may hold values from -360 to 360
- cached_values: bfloat16 [192, 8, 3456, 128], P('req', 'tp'), may hold values from -24 to 24
- cache_lengths: int32 [192], P('req'), may hold values from 864 to 3456, as said below
- tree_parent: int32 [192, 64], P('req'), may hold values from 0 to 63, as said below
- kept_nodes: int32 [192, 8], P('req'), may hold values from 0 to 63
Outputs:
- layer_out: bfloat16 [192, 64, 3072], P('req', None, 'tp')
- appended: bfloat16 [192, 2, 8, 8, 128], P('req', None, None, 'tp')
Inputs may be any that keep to these rules, and one draw needn't show every extreme that they name: `request_order`: each request is held by exactly one slot. The 6 requests of one device's rows go to 6 different devices of req, and the slots of one device hold requests of 6 different devices. `cache_lengths`: some slot has exactly 3456 live positions. `tree_parent`: node 0 has parent 0; every other node's parent has a lower index.
All inputs are finite; a program needn't handle non-finite values.
Results may differ from a plain program's by a relative error of at most 0.0085.
The roundings to bfloat16 on the way count: a program that leaves them out, or rounds other values in their place, can miss the bound.
Values may be sent and summed in bfloat16 or wider, within the bound.
A program may use at most 128 MiB of HBM per device.

v0:
```python
import jax
import jax.numpy as jnp
from jax import lax
from jax.sharding import PartitionSpec as P

HEAD_WIDTH = 128
NORM_EPSILON = 1e-05


def rotary_embedding(vectors, token_positions):
    half_dim = vectors.shape[-1] // 2
    frequency = 500000.0 ** (-jnp.arange(half_dim, dtype=jnp.float32) * 2.0 / vectors.shape[-1])
    angles = token_positions[..., None] * frequency
    cosine = jnp.cos(angles)[..., None, :]
    sine = jnp.sin(angles)[..., None, :]
    first_half = vectors[..., :half_dim]
    second_half = vectors[..., half_dim:]
    return jnp.concatenate(
        [first_half * cosine - second_half * sine, second_half * cosine + first_half * sine],
        axis=-1,
    )


def body(
    hidden_in,
    request_order,
    norm_gain,
    w_query,
    key_weight,
    value_weight,
    w_out,
    key_cache,
    cached_values,
    cache_lengths,
    tree_parent,
    kept_nodes,
):
    slots_here = key_cache.shape[0]
    tree_length = hidden_in.shape[1]
    width_local = hidden_in.shape[2]
    local_groups = key_cache.shape[1]
    local_heads = w_query.shape[1] // HEAD_WIDTH
    group_width = local_heads // local_groups
    slot_ids = lax.axis_index("req") * slots_here + jnp.arange(slots_here, dtype=jnp.int32)
    own_order = request_order[slot_ids]
    piece = lax.all_gather(hidden_in, "req", axis=0, tiled=True)
    piece_ids = jnp.arange(piece.shape[0], dtype=jnp.int32)
    chooser = (own_order[:, None] == piece_ids[None, :]).astype(jnp.bfloat16)
    dealt = jnp.einsum("rm,mtd->rtd", chooser, piece, preferred_element_type=jnp.float32).astype(
        jnp.bfloat16
    )
    widened = lax.all_gather(dealt, "tp", axis=2, tiled=True).astype(jnp.float32)
    normalized_input = (
        widened
        * lax.rsqrt(jnp.mean(widened * widened, axis=-1, keepdims=True) + NORM_EPSILON)
        * norm_gain.astype(jnp.float32)
    ).astype(jnp.bfloat16)
    flat_rows = normalized_input.reshape(slots_here * tree_length, normalized_input.shape[2])
    query_rows = jnp.dot(flat_rows, w_query, preferred_element_type=jnp.float32).reshape(
        slots_here, tree_length, local_heads, HEAD_WIDTH
    )
    fresh_keys = jnp.dot(flat_rows, key_weight, preferred_element_type=jnp.float32).reshape(
        slots_here, tree_length, local_groups, HEAD_WIDTH
    )
    fresh_values = (
        jnp.dot(flat_rows, value_weight, preferred_element_type=jnp.float32)
        .astype(jnp.bfloat16)
        .reshape(slots_here, tree_length, local_groups, HEAD_WIDTH)
    )
    node_ids = jnp.arange(tree_length, dtype=jnp.int32)
    parent_link = (
        (tree_parent[:, :, None] == node_ids[None, None, :]) & (node_ids[None, :, None] > 0)
    ).astype(jnp.float32)
    ancestry = jnp.eye(tree_length, dtype=jnp.float32)[None] + parent_link
    for sweep in range(tree_length.bit_length()):
        ancestry = jnp.minimum(
            jnp.einsum("rij,rjk->rik", ancestry, ancestry, precision=lax.Precision.HIGHEST), 1.0
        )
    token_positions = cache_lengths.astype(jnp.float32)[:, None] + jnp.sum(ancestry, axis=-1) - 1.0
    rotated_query = (
        rotary_embedding(query_rows, token_positions)
        .astype(jnp.bfloat16)
        .reshape(slots_here, tree_length, local_groups, group_width, HEAD_WIDTH)
    )
    key_rot = rotary_embedding(fresh_keys, token_positions).astype(jnp.bfloat16)
    score_scale = HEAD_WIDTH ** (-0.5)
    cache_scores = (
        jnp.einsum(
            "rtgqd,rgcd->rgqtc", rotated_query, key_cache, preferred_element_type=jnp.float32
        )
        * score_scale
    )
    live_keys = jnp.arange(key_cache.shape[2], dtype=jnp.int32)[None, :] < cache_lengths[:, None]
    cache_scores = jnp.where(live_keys[:, None, None, None, :], cache_scores, -jnp.inf)
    tree_scores = (
        jnp.einsum("rtgqd,rsgd->rgqts", rotated_query, key_rot, preferred_element_type=jnp.float32)
        * score_scale
    )
    tree_scores = jnp.where(ancestry[:, None, None] > 0, tree_scores, -jnp.inf)
    row_max = jnp.maximum(jnp.max(cache_scores, axis=-1), jnp.max(tree_scores, axis=-1))
    cache_exp = jnp.exp(cache_scores - row_max[..., None])
    tree_exp = jnp.exp(tree_scores - row_max[..., None])
    row_total = jnp.sum(cache_exp, axis=-1) + jnp.sum(tree_exp, axis=-1)
    cache_weights = (cache_exp / row_total[..., None]).astype(jnp.bfloat16)
    tree_weights = (tree_exp / row_total[..., None]).astype(jnp.bfloat16)
    attended = jnp.einsum(
        "rgqtc,rgcd->rtgqd", cache_weights, cached_values, preferred_element_type=jnp.float32
    )
    attended = attended + jnp.einsum(
        "rgqts,rsgd->rtgqd", tree_weights, fresh_values, preferred_element_type=jnp.float32
    )
    attended = attended.astype(jnp.bfloat16).reshape(
        slots_here, tree_length, local_heads * HEAD_WIDTH
    )
    keep_select = (kept_nodes[:, :, None] == node_ids[None, None, :]).astype(jnp.bfloat16)
    stacked = jnp.stack([key_rot, fresh_values], axis=1)
    appended = jnp.einsum(
        "rkt,rxtgd->rxkgd", keep_select, stacked, preferred_element_type=jnp.float32
    ).astype(jnp.bfloat16)
    partials = jnp.dot(
        attended.reshape(-1, attended.shape[2]), w_out, preferred_element_type=jnp.float32
    )
    summed = lax.psum(partials, "tp")
    my_share = lax.dynamic_slice_in_dim(summed, lax.axis_index("tp") * width_local, width_local, 1)
    layer_out = (my_share.reshape(dealt.shape) + dealt.astype(jnp.float32)).astype(jnp.bfloat16)
    return (layer_out, appended)


def solution(mesh):
    placed = (
        P("req", None, "tp"),
        P(),
        P(),
        P(None, "tp"),
        P(None, "tp"),
        P(None, "tp"),
        P("tp", None),
        P("req", "tp", None, None),
        P("req", "tp", None, None),
        P("req"),
        P("req", None),
        P("req", None),
    )
    return jax.shard_map(
        body,
        mesh=mesh,
        in_specs=placed,
        out_specs=(P("req", None, "tp"), P("req", None, None, "tp", None)),
        check_vma=False,
    )
```

profile of v0, /device:TPU:2, one launch (start us, length us, event | category | flops | bytes accessed | tf_op | source)
XLA Modules:
  0.0 284.8 jit_solution(10960639715566622475)
XLA Ops:
  7.2 0.7 all-gather.3.cloned.1.call-update
  8.0 1.3 gather_fusion
  9.3 106.1 %all-gather.3.cloned.1.call-done = bf16[192,64,384]{2,1,0:T(8,128)(2,1)} async-done(((bf16[6,64,384]{2,1,0:T(8,128)(2,1)}), bf16[192,64,384]{2,1,0:T(8,128)(2,1)}) %all-gather.3.cloned.1.call-update) | async-done | bytes 9437200 | tf_op jit(solution)/shard_map/all_gather | solution.py:46
  115.4 11.9 %fusion.3 = bf16[6,64,384]{2,0,1:T(8,128)(2,1)S(1)} fusion(bf16[192,64,384]{2,1,0:T(8,128)(2,1)} %all-gather.3.cloned.1.call-done, s32[6]{0:T(128)S(1)} %gather_fusion), kind=kOutput, calls=%fused_computation.7 | convolution fusion | flops 56624256 | bytes 9732120 | tf_op jit(solution)/shard_map/rm,mtd->rtd/dot_general | solution.py:49
  127.3 0.8 copy.78
  128.3 0.5 convolution_minimum_fusion.6
  131.0 4.5 %copy.51 = bf16[3072,384]{0,1:T(8,128)(2,1)} copy(bf16[3072,384]{1,0:T(8,128)(2,1)} %param.15) | data formatting | bytes 4718592 | tf_op args[3]
  135.5 0.8 multiply_cosine_fusion.1
  136.4 19.0 %all-gather.5.cloned.1.call-done = bf16[6,64,3072]{2,1,0:T(8,128)(2,1)} async-done(((bf16[6,64,384]{2,1,0:T(8,128)(2,1)}), bf16[6,64,3072]{2,1,0:T(8,128)(2,1)}) %all-gather.5.cloned.1.call-update) | async-done | bytes 2359312 | tf_op jit(solution)/shard_map/all_gather | solution.py:52
  155.4 2.4 fusion.11
  157.7 2.4 fusion.13
  160.2 0.8 convolution_bitcast_fusion
  161.0 0.8 fusion.38
  161.8 1.4 fusion.14
  163.6 6.9 %fusion.2 = (f32[6,3,64]{2,1,0:T(4,128)S(1)}, f32[6,64,3,3456]{3,1,2,0:T(8,128)}) fusion(pred[6,3456]{1,0:T(8,128)(4,1)S(1)} %iota_compare_fusion.1, bf16[6,1,3456,128]{3,2,1,0:T(8,128)(2,1)S(1)} %bitcast.146, bf16[6,64,3,64]{3,1,2,0:T(8,128)(2,1)S(1)} %get-tuple-element.11, bf16[6,64,3,64]{3,1,2,0:T(8,128)(2,1)S(1)} %get-tuple-element.10), kind=kOutput, calls=%fused_computation.6 | convolution fusion | flops 1031748480 | bytes 21553920 | tf_op jit(solution)/shard_map/rtgqd,rgcd->rgqtc/dot_general | solution.py:88
  170.5 0.4 fusion.64
  171.1 9.2 %fusion.1 = f32[6,3,64]{2,1,0:T(4,128)S(1)} fusion(f32[6,64,3,3456]{3,1,2,0:T(8,128)} %get-tuple-element.19, f32[6,3,64]{2,1,0:T(4,128)S(1)} %max.9, pred[6,3456]{1,0:T(8,128)(4,1)S(1)} %iota_compare_fusion.1), kind=kLoop, calls=%fused_computation.5 | loop fusion | flops 15924096 | bytes 15955200 | tf_op jit(solution)/shard_map/reduce_sum | solution.py:103
  180.3 1.9 convolution_convert_fusion
  182.2 10.3 %fusion.17 = f32[6,128,3,64]{1,3,2,0:T(8,128)S(1)} fusion(bf16[6,1,3456,128]{3,2,1,0:T(8,128)(2,1)} %param.20, f32[6,3,64]{2,1,0:T(4,128)S(1)} %add.98, f32[6,3,64]{2,1,0:T(4,128)S(1)} %max.9, f32[6,64,3,3456]{3,1,2,0:T(8,128)} %get-tuple-element.19, pred[6,3456]{1,0:T(8,128)(4,1)S(1)} %iota_compare_fusion.1), kind=kOutput, calls=%fused_computation.25 | convolution fusion | flops 1039122432 | bytes 21853440 | tf_op jit(solution)/shard_map/rgqtc,rgcd->rtgqd/dot_general | solution.py:106
  193.1 3.5 %fusion.28 = f32[384,3072]{1,0:T(8,128)} fusion(bf16[384,3072]{1,0:T(8,128)(2,1)S(1)} %copy-done, bf16[48,8,3,128]{3,2,1,0:T(4,128)(2,1)S(1)} %bitcast.149), kind=kOutput, calls=%fused_computation.48 | convolution fusion | flops 905969664 | bytes 7372800 | tf_op jit(solution)/shard_map/dot_general | solution.py:120
  196.7 0.8 fusion.25
  197.5 78.8 %all-reduce.2.cloned.1.call-done = f32[384,3072]{1,0:T(8,128)} async-done(((f32[384,3072]{1,0:T(8,128)}), f32[384,3072]{1,0:T(8,128)}) %all-reduce.2.cloned.1.call-update) | async-done | bytes 4718608 | tf_op jit(solution)/shard_map/psum | solution.py:123
  276.3 1.1 constant_dynamic-slice_fusion
  277.4 0.8 add_convert_fusion
  (48 shorter events, 3.6 us)
Async XLA Ops:
  7.2 185.9 %copy-start = (bf16[384,3072]{1,0:T(8,128)(2,1)S(1)}, bf16[384,3072]{1,0:T(8,128)(2,1)}, u32[]{:S(2)}) copy-start(bf16[384,3072]{1,0:T(8,128)(2,1)} %param.18) | copy-start | bytes 7077892
  7.2 108.2 %all-gather.3.cloned.1.call-start = ((), (), s32[]{:S(2)}) async-start(), calls=%async_computation | async-start | bytes 9732096 | tf_op jit(solution)/shard_map/all_gather | solution.py:46
  7.9 147.5 %all-gather.5.cloned.1.call-start = ((), (), s32[]{:S(2)}) async-start(), calls=%async_computation.1 | async-start | bytes 2654208 | tf_op jit(solution)/shard_map/all_gather | solution.py:52
  9.3 118.9 %copy-start.4 = (s32[6]{0:T(128)S(1)}, s32[6]{0:T(128)}, u32[]{:S(2)}) copy-start(s32[6]{0:T(128)} %param.21) | copy-start | bytes 76
  9.3 118.9 %copy-start.3 = (bf16[3072]{0:T(1024)(128)(2,1)S(1)}, bf16[3072]{0:T(1024)(128)(2,1)}, u32[]{:S(2)}) copy-start(bf16[3072]{0:T(1024)(128)(2,1)} %param.14) | copy-start | bytes 18436
  9.3 118.9 %copy-start.5 = (s32[6,64]{1,0:T(8,128)S(1)}, s32[6,64]{1,0:T(8,128)}, u32[]{:S(2)}) copy-start(s32[6,64]{1,0:T(8,128)} %param.22) | copy-start | bytes 4612
  128.1 148.2 %all-reduce.2.cloned.1.call-start = ((), (), s32[]{:S(2)}) async-start(), calls=%async_computation.2 | async-start | bytes 9437184 | tf_op jit(solution)/shard_map/psum | solution.py:123
  155.4 4.8 %copy-start.2 = (bf16[3072,128]{1,0:T(8,128)(2,1)S(1)}, bf16[3072,128]{1,0:T(8,128)(2,1)}, u32[]{:S(2)}) copy-start(bf16[3072,128]{1,0:T(8,128)(2,1)} %param.16) | copy-start | bytes 2359300
  155.4 6.4 %copy-start.1 = (bf16[3072,384]{0,1:T(8,128)(2,1)S(1)}, bf16[3072,384]{0,1:T(8,128)(2,1)}, u32[]{:S(2)}) copy-start(bf16[3072,384]{0,1:T(8,128)(2,1)} %copy.51) | copy-start | bytes 7077892
  160.2 3.4 %slice-start = ((s8[5308416]{0:T(1024)(128)(4,1)}), s8[4194304]{0:T(1024)(128)(4,1)S(1)}, s32[]{:S(2)}) async-start(s8[5308416]{0:T(1024)(128)(4,1)} %bitcast.145), calls=%async_computation.3 | async-start | bytes 8388608
  161.8 1.7 slice-start.1
  193.1 3.6 %copy-start.6 = (s32[6,8]{1,0:T(8,128)S(1)}, s32[6,8]{1,0:T(8,128)}, u32[]{:S(2)}) copy-start(s32[6,8]{1,0:T(8,128)} %param.23) | copy-start | bytes 580
Sparse Core Ops, SparseCore 0:
  10.6 104.8 all-gather.2
  128.2 27.0 all-gather.4
  196.8 79.4 all-reduce.1
where the time goes:
time: 285 us
  waiting for transfers between devices  205 us (72%)
  matrix products  40.8 us (14%)
  other arithmetic  17 us (6%)
  between operations  14.1 us (5%)
  local copies, waits for them, and re-layouts  8.1 us (3%)
    all_gather x1, waiting for transfers between devices, body(): piece = lax.all_gather(hidden_in, 'req', axis=0, tiled=True)  106 us
    psum x1, waiting for transfers between devices, body(): summed = lax.psum(partials, 'tp')  78.8 us
    all_gather x1, waiting for transfers between devices, body(): lax.all_gather(dealt, 'tp', axis=2, tiled=True).astype(jnp.float32)  19 us
    dot_general x1, matrix products, body(): jnp.einsum('rm,mtd->rtd', chooser, piece, preferred_element_type=jnp.floa...  11.9 us
    dot_general x1, matrix products, body(): jnp.einsum('rgqtc,rgcd->rtgqd', cache_weights, cached_values, preferred_e...  10.3 us
    reduce_sum x2, other arithmetic, body(): row_total = jnp.sum(cache_exp, axis=-1) + jnp.sum(tree_exp, axis=-1)  9.32 us
    dot_general x1, matrix products, body(): jnp.einsum('rtgqd,rgcd->rgqtc', rotated_query, key_cache, preferred_eleme...  6.91 us
  transfers between devices with their start and end apart: 3, of which 3 were waited for; matrix products, arithmetic and copies ran while one was open for 4% of the time, Pallas kernels for 0%

commit v1 on v0

--- a/solution.py
+++ b/solution.py
@@ -120,7 +120,8 @@
     partials = jnp.dot(
         attended.reshape(-1, attended.shape[2]), w_out, preferred_element_type=jnp.float32
     )
-    summed = lax.psum(partials, "tp")
+    divide_leaf = lambda t0: jnp.sum(lax.all_gather(t0, "tp"), axis=0)
+    summed = divide_leaf(partials)
     my_share = lax.dynamic_slice_in_dim(summed, lax.axis_index("tp") * width_local, width_local, 1)
     layer_out = (my_share.reshape(dealt.shape) + dealt.astype(jnp.float32)).astype(jnp.bfloat16)
     return (layer_out, appended)

time: 285 us -> 401 us (1.41)
  waiting for transfers between devices: 205 us -> 303 us
  other arithmetic: 17 us -> 33.5 us
    all_gather x0 -> x1, waiting for transfers between devices: none -> 177 us  [body(): divide_leaf = lambda t0: jnp.sum(lax.all_gather(t0, 'tp'), axis=0)]
    psum x1 -> x0, waiting for transfers between devices: 78.8 us -> none  [body(): summed = lax.psum(partials, 'tp')]
    reduce_sum x0 -> x1, other arithmetic: none -> 16.4 us  [body(): divide_leaf = lambda t0: jnp.sum(lax.all_gather(t0, 'tp'), axis=0)]
  transfers between devices with their start and end apart: 3 -> 3, of which waited for: 3 -> 3; matrix products, arithmetic and copies ran while one was open for 4% -> 3% of each run, Pallas kernels for 0% -> 0%
where the time goes in v1:
time: 401 us; the launch traced here: 400 us
  waiting for transfers between devices  303 us (76%)
  matrix products  40.9 us (10%)
  other arithmetic  33.5 us (8%)
  between operations  14.2 us (4%)
  local copies, waits for them, and re-layouts  8.11 us (2%)
    all_gather x1, waiting for transfers between devices, body(): divide_leaf = lambda t0: jnp.sum(lax.all_gather(t0, 'tp'), axis=0)  177 us
    all_gather x1, waiting for transfers between devices, body(): piece = lax.all_gather(hidden_in, 'req', axis=0, tiled=True)  106 us
    all_gather x1, waiting for transfers between devices, body(): lax.all_gather(dealt, 'tp', axis=2, tiled=True).astype(jnp.float32)  19 us
    reduce_sum x1, other arithmetic, body(): divide_leaf = lambda t0: jnp.sum(lax.all_gather(t0, 'tp'), axis=0)  16.4 us
    dot_general x1, matrix products, body(): jnp.einsum('rm,mtd->rtd', chooser, piece, preferred_element_type=jnp.floa...  11.9 us
    dot_general x1, matrix products, body(): jnp.einsum('rgqtc,rgcd->rtgqd', cache_weights, cached_values, preferred_e...  10.3 us
    reduce_sum x2, other arithmetic, body(): row_total = jnp.sum(cache_exp, axis=-1) + jnp.sum(tree_exp, axis=-1)  9.32 us
  transfers between devices with their start and end apart: 3, of which 3 were waited for; matrix products, arithmetic and copies ran while one was open for 3% of the time, Pallas kernels for 0%

profile of v1, /device:TPU:2, one launch (start us, length us, event | category | flops | bytes accessed | tf_op | source)
XLA Modules:
  0.0 399.6 jit_solution(16269905921644281772)
XLA Ops:
  7.2 0.7 all-gather.5.cloned.1.call-update
  8.0 1.3 gather_fusion
  9.3 106.1 %all-gather.5.cloned.1.call-done = bf16[192,64,384]{2,1,0:T(8,128)(2,1)} async-done(((bf16[6,64,384]{2,1,0:T(8,128)(2,1)}), bf16[192,64,384]{2,1,0:T(8,128)(2,1)}) %all-gather.5.cloned.1.call-update) | async-done | bytes 9437200 | tf_op jit(solution)/shard_map/all_gather | solution.py:46
  115.4 11.9 %fusion.3 = bf16[6,64,384]{2,0,1:T(8,128)(2,1)S(1)} fusion(bf16[192,64,384]{2,1,0:T(8,128)(2,1)} %all-gather.5.cloned.1.call-done, s32[6]{0:T(128)S(1)} %gather_fusion), kind=kOutput, calls=%fused_computation.7 | convolution fusion | flops 56624256 | bytes 9732120 | tf_op jit(solution)/shard_map/rm,mtd->rtd/dot_general | solution.py:49
  127.3 0.8 copy.78
  128.2 0.5 convolution_minimum_fusion.6
  131.0 4.5 %copy.51 = bf16[3072,384]{0,1:T(8,128)(2,1)} copy(bf16[3072,384]{1,0:T(8,128)(2,1)} %param.15) | data formatting | bytes 4718592 | tf_op args[3]
  135.5 0.8 multiply_cosine_fusion.1
  136.4 19.0 %all-gather.7.cloned.1.call-done = bf16[6,64,3072]{2,1,0:T(8,128)(2,1)} async-done(((bf16[6,64,384]{2,1,0:T(8,128)(2,1)}), bf16[6,64,3072]{2,1,0:T(8,128)(2,1)}) %all-gather.7.cloned.1.call-update) | async-done | bytes 2359312 | tf_op jit(solution)/shard_map/all_gather | solution.py:52
  155.4 2.4 fusion.11
  157.7 2.4 fusion.13
  160.2 0.8 convolution_bitcast_fusion
  161.0 0.8 fusion.38
  161.9 1.4 fusion.14
  163.6 6.9 %fusion.2 = (f32[6,3,64]{2,1,0:T(4,128)S(1)}, f32[6,64,3,3456]{3,1,2,0:T(8,128)}) fusion(pred[6,3456]{1,0:T(8,128)(4,1)S(1)} %iota_compare_fusion.1, bf16[6,1,3456,128]{3,2,1,0:T(8,128)(2,1)S(1)} %bitcast.148, bf16[6,64,3,64]{3,1,2,0:T(8,128)(2,1)S(1)} %get-tuple-element.11, bf16[6,64,3,64]{3,1,2,0:T(8,128)(2,1)S(1)} %get-tuple-element.10), kind=kOutput, calls=%fused_computation.6 | convolution fusion | flops 1031748480 | bytes 21553920 | tf_op jit(solution)/shard_map/rtgqd,rgcd->rgqtc/dot_general | solution.py:88
  171.1 9.2 %fusion.1 = f32[6,3,64]{2,1,0:T(4,128)S(1)} fusion(f32[6,64,3,3456]{3,1,2,0:T(8,128)} %get-tuple-element.19, f32[6,3,64]{2,1,0:T(4,128)S(1)} %max.9, pred[6,3456]{1,0:T(8,128)(4,1)S(1)} %iota_compare_fusion.1), kind=kLoop, calls=%fused_computation.5 | loop fusion | flops 15924096 | bytes 15955200 | tf_op jit(solution)/shard_map/reduce_sum | solution.py:103
  180.3 1.9 convolution_convert_fusion
  182.2 10.3 %fusion.17 = f32[6,128,3,64]{1,3,2,0:T(8,128)S(1)} fusion(bf16[6,1,3456,128]{3,2,1,0:T(8,128)(2,1)} %param.20, f32[6,3,64]{2,1,0:T(4,128)S(1)} %add.96, f32[6,3,64]{2,1,0:T(4,128)S(1)} %max.9, f32[6,64,3,3456]{3,1,2,0:T(8,128)} %get-tuple-element.19, pred[6,3456]{1,0:T(8,128)(4,1)S(1)} %iota_compare_fusion.1), kind=kOutput, calls=%fused_computation.25 | convolution fusion | flops 1039122432 | bytes 21853440 | tf_op jit(solution)/shard_map/rgqtc,rgcd->rtgqd/dot_general | solution.py:106
  193.2 3.6 fusion.28
  196.8 0.8 fusion.25
  197.7 177.1 %all-gather.9.cloned.1.call-done = f32[3072,3072]{1,0:T(8,128)} async-done(((f32[384,3072]{1,0:T(8,128)}), f32[3072,3072]{1,0:T(8,128)}) %all-gather.9.cloned.1.call-update) | async-done | bytes 37748752 | tf_op jit(solution)/shard_map/all_gather | solution.py:123
  374.7 16.4 %reduce_sum.49 = f32[384,3072]{1,0:T(8,128)} reduce(f32[8,384,3072]{2,1,0:T(8,128)} %bitcast.145, f32[]{:T(128)} %constant.7.clone.1), dimensions={0}, to_apply=%region_6.7 | reduce | flops 8257536 | bytes 42467332 | tf_op jit(solution)/shard_map/reduce_sum | solution.py:123
  391.2 1.1 constant_dynamic-slice_fusion
  392.3 0.8 add_convert_fusion
  (57 shorter events, 4.1 us)
Async XLA Ops:
  7.2 186.0 %copy-start = (bf16[384,3072]{1,0:T(8,128)(2,1)S(1)}, bf16[384,3072]{1,0:T(8,128)(2,1)}, u32[]{:S(2)}) copy-start(bf16[384,3072]{1,0:T(8,128)(2,1)} %param.18) | copy-start | bytes 7077892
  7.2 108.2 %all-gather.5.cloned.1.call-start = ((), (), s32[]{:S(2)}) async-start(), calls=%async_computation | async-start | bytes 9732096 | tf_op jit(solution)/shard_map/all_gather | solution.py:46
  7.9 147.5 %all-gather.7.cloned.1.call-start = ((), (), s32[]{:S(2)}) async-start(), calls=%async_computation.1 | async-start | bytes 2654208 | tf_op jit(solution)/shard_map/all_gather | solution.py:52
  9.3 118.9 %copy-start.6 = (s32[6]{0:T(128)S(1)}, s32[6]{0:T(128)}, u32[]{:S(2)}) copy-start(s32[6]{0:T(128)} %param.21) | copy-start | bytes 76
  9.3 118.9 %copy-start.5 = (bf16[3072]{0:T(1024)(128)(2,1)S(1)}, bf16[3072]{0:T(1024)(128)(2,1)}, u32[]{:S(2)}) copy-start(bf16[3072]{0:T(1024)(128)(2,1)} %param.14) | copy-start | bytes 18436
  9.3 118.9 %copy-start.7 = (s32[6,64]{1,0:T(8,128)S(1)}, s32[6,64]{1,0:T(8,128)}, u32[]{:S(2)}) copy-start(s32[6,64]{1,0:T(8,128)} %param.22) | copy-start | bytes 4612
  128.1 246.6 %all-gather.9.cloned.1.call-start = ((), (), s32[]{:S(2)}) async-start(), calls=%async_computation.2 | async-start | bytes 42467328 | tf_op jit(solution)/shard_map/all_gather | solution.py:123
  155.4 4.8 %copy-start.2 = (bf16[3072,128]{1,0:T(8,128)(2,1)S(1)}, bf16[3072,128]{1,0:T(8,128)(2,1)}, u32[]{:S(2)}) copy-start(bf16[3072,128]{1,0:T(8,128)(2,1)} %param.16) | copy-start | bytes 2359300
  155.4 6.5 %copy-start.1 = (bf16[3072,384]{0,1:T(8,128)(2,1)S(1)}, bf16[3072,384]{0,1:T(8,128)(2,1)}, u32[]{:S(2)}) copy-start(bf16[3072,384]{0,1:T(8,128)(2,1)} %copy.51) | copy-start | bytes 7077892
  160.2 3.4 slice-start
  161.8 8.7 %copy-start.3 = (bf16[6,64,1,64]{3,1,0,2:T(8,128)(2,1)}, bf16[6,64,1,64]{3,1,0,2:T(8,128)(2,1)S(1)}, u32[]{:S(2)}) copy-start(bf16[6,64,1,64]{3,1,0,2:T(8,128)(2,1)S(1)} %get-tuple-element.13) | copy-start | bytes 147460
  161.8 1.7 slice-start.1
  182.2 10.4 %copy-start.9 = (bf16[384,128]{1,0:T(8,128)(2,1)}, bf16[384,128]{1,0:T(8,128)(2,1)S(1)}, u32[]{:S(2)}) copy-start(bf16[384,128]{1,0:T(8,128)(2,1)S(1)} %convolution_convert_fusion) | copy-start | bytes 294916
  193.2 3.6 copy-start.4
  193.2 3.6 copy-start.8
  193.2 3.6 copy-start.10
Sparse Core Ops, SparseCore 0:
  10.6 104.8 all-gather.4
  128.2 27.0 all-gather.6
  196.9 177.7 all-gather.8
